TPU v7x, 32 devices: a whole 2x2x4 slice. The times are simulated.
32 devices in a mesh: groups: 2 (over x), seq: 16 (over z, y, core).
Axes of the slice: x: 2, y: 2, z: 4, core: 2. Of those that a mesh axis runs over, the one named last changes fastest.
Arguments:
- queries: bfloat16 [4096, 2048], P(('groups', 'seq')), parts along dimension 0, may hold values from -140 to 140
- keys: bfloat16 [4096, 2048], P(('groups', 'seq')), parts along dimension 0, may hold values from -6.25 to 6.25
- values: bfloat16 [4096, 2048], P(('groups', 'seq')), parts along dimension 0, may hold values from -6 to 6
- grad_out: bfloat16 [4096, 2048], P(('groups', 'seq')), parts along dimension 0, may hold values from -6 to 6
- partners: int32 [32, 16, 3], P(('groups', 'seq')), parts along dimension 0, may hold values from 0 to 15, all different within a row; in each aligned block of 16 rows (0 to 15, 16 to 31, ..., all dimensions but the last counted through in order) at most 3 rows name the same one
Outputs:
- grad_queries: bfloat16 [4096, 2048], P(('groups', 'seq')), parts along dimension 0
- grad_keys: bfloat16 [4096, 2048], P(('groups', 'seq')), parts along dimension 0
- grad_values: bfloat16 [4096, 2048], P(('groups', 'seq')), parts along dimension 0
There are 2 independent parts, one for each index of `groups`. A program takes and returns all parts, laid end to end along the dimension named above; each array names one. Nothing has to cross between parts.
Inputs may be any that keep to these rules, and one draw needn't show every extreme that they name: In the 16 head rows of one query block, no block is named more than 3 times, and some block is named exactly 3 times; the 3 partners of one head are different blocks.
All inputs are finite; a program needn't handle non-finite values.
Results may differ from a plain program's by a relative error of at most 0.01.
Values may be sent and summed in bfloat16 or wider, within the bound.
A program may use at most 128 MiB of HBM per device.

v0:
```python
import math
import jax
import jax.numpy as jnp
from jax import lax
from jax.sharding import PartitionSpec as P

H = 16
HD = 128


def with_halo(shard, sides, width):
    for axis, dim in sides:
        count, length = (lax.axis_size(axis), shard.shape[dim])
        up = [(i, (i + 1) % count) for i in range(count - 1)]
        down = [(j, i) for i, j in up]
        last = lax.slice_in_dim(shard, length - width, length, axis=dim)
        first = lax.slice_in_dim(shard, 0, width, axis=dim)
        before = lax.ppermute(last, axis, up)
        after = lax.ppermute(first, axis, down)
        shard = jnp.concatenate([before, shard, after], axis=dim)
    return shard


def broadcast(block, axis, source):
    block = jnp.where(lax.axis_index(axis) == source, block, jnp.zeros_like(block))
    return lax.psum(block, axis)


def per_device(queries, keys, values, grad_out, partners):
    devices = lax.axis_size("seq")
    my_index = lax.axis_index("seq")
    most_slots = max(2, (3 * H + devices - 1) // devices)
    softmax_scale = 1.0 / math.sqrt(HD)
    width = H * HD
    rows_here = queries.shape[0]
    kv_local = jnp.stack([keys, values])
    query_heads = queries.reshape(rows_here, H, HD)
    grad_heads = grad_out.reshape(rows_here, H, HD)
    lower_ok = my_index > 0
    upper_ok = my_index < devices - 1
    window = with_halo(kv_local, (("seq", 1),), rows_here)
    sink_parts = [broadcast(kv_local, "seq", sink_root) for sink_root in range(2)]
    near_kv = jnp.concatenate([window] + sink_parts, axis=1).reshape(2, 5 * rows_here, H, HD)
    near_keys = near_kv[0]
    near_values = near_kv[1]
    item_count = 3 * H
    dests = partners.reshape(item_count)
    item_heads = jnp.arange(item_count, dtype=jnp.int32) // 3
    dest_hot = (dests[:, None] == jnp.arange(devices, dtype=jnp.int32)[None, :]).astype(jnp.int32)
    slot_rank = jnp.sum((jnp.cumsum(dest_hot, axis=0) - dest_hot) * dest_hot, axis=1)
    kv_by_head = kv_local.reshape(2, rows_here, H, HD).transpose(2, 0, 1, 3)
    requests = jnp.full((devices, most_slots), -1, jnp.int32).at[dests, slot_rank].set(item_heads)
    wanted = lax.all_to_all(requests, "seq", split_axis=0, concat_axis=0, tiled=True)
    picked = kv_by_head[jnp.maximum(wanted, 0)]
    fetched = lax.all_to_all(
        jnp.where((wanted >= 0)[:, :, None, None, None], picked, jnp.zeros_like(picked)),
        "seq",
        split_axis=0,
        concat_axis=0,
        tiled=True,
    )
    far_kv = fetched[dests, slot_rank].reshape(H, 3, 2, rows_here, HD)
    far_keys = far_kv[:, :, 0]
    far_values = far_kv[:, :, 1]
    near_scores = softmax_scale * jnp.einsum(
        "thd,khd->htk", query_heads, near_keys, preferred_element_type=jnp.float32
    )
    far_scores = softmax_scale * jnp.einsum(
        "thd,hrkd->htrk", query_heads, far_keys, preferred_element_type=jnp.float32
    )
    key_pos = jnp.arange(5 * rows_here, dtype=jnp.int32)
    key_ok = jnp.logical_not((key_pos < rows_here) & jnp.logical_not(lower_ok))
    key_ok = key_ok & jnp.logical_not(
        (key_pos >= 2 * rows_here) & (key_pos < 3 * rows_here) & jnp.logical_not(upper_ok)
    )
    near_max = jnp.max(
        jnp.where(key_ok[None, None, :], near_scores, -jnp.inf), axis=2, keepdims=True
    )
    far_max = jnp.max(far_scores, axis=(2, 3))[:, :, None]
    row_max = jnp.maximum(near_max, far_max)
    near_total = jnp.sum(
        jnp.where(key_ok[None, None, :], jnp.exp(near_scores - row_max), 0.0), axis=2, keepdims=True
    )
    far_total = jnp.sum(jnp.exp(far_scores - row_max[:, :, :, None]), axis=(2, 3))[:, :, None]
    totals = near_total + far_total

    def near_prob_f32():
        return jnp.where(key_ok[None, None, :], jnp.exp(near_scores - row_max), 0.0) / totals

    def far_prob_f32():
        return jnp.exp(far_scores - row_max[:, :, :, None]) / totals[:, :, :, None]

    near_probs = near_prob_f32().astype(jnp.bfloat16)
    far_probs = far_prob_f32().astype(jnp.bfloat16)
    attended = jnp.einsum(
        "htk,khd->htd", near_probs, near_values, preferred_element_type=jnp.float32
    )
    attended = attended + jnp.einsum(
        "htrk,hrkd->htd", far_probs, far_values, preferred_element_type=jnp.float32
    )
    delta = jnp.sum(grad_heads.transpose(1, 0, 2) * attended, axis=2)
    near_dprob = jnp.einsum(
        "thd,khd->htk", grad_heads, near_values, preferred_element_type=jnp.float32
    )
    far_dprob = jnp.einsum(
        "thd,hrkd->htrk", grad_heads, far_values, preferred_element_type=jnp.float32
    )
    near_dscore = (near_prob_f32() * (near_dprob - delta[:, :, None])).astype(jnp.bfloat16)
    far_dscore = (far_prob_f32() * (far_dprob - delta[:, :, None, None])).astype(jnp.bfloat16)
    grad_q = jnp.einsum("htk,khd->thd", near_dscore, near_keys, preferred_element_type=jnp.float32)
    grad_q = grad_q + jnp.einsum(
        "htrk,hrkd->thd", far_dscore, far_keys, preferred_element_type=jnp.float32
    )
    grad_queries = (softmax_scale * grad_q).reshape(rows_here, width).astype(jnp.bfloat16)
    near_key_term = softmax_scale * jnp.einsum(
        "htk,thd->khd", near_dscore, query_heads, preferred_element_type=jnp.float32
    )
    near_value_term = jnp.einsum(
        "htk,thd->khd", near_probs, grad_heads, preferred_element_type=jnp.float32
    )
    near_terms = jnp.stack(
        [near_key_term.reshape(5 * rows_here, width), near_value_term.reshape(5 * rows_here, width)]
    )
    own_grads = near_terms[:, rows_here : 2 * rows_here]
    outgoing = jnp.concatenate(
        [near_terms[:, :rows_here], near_terms[:, 2 * rows_here : 3 * rows_here]], axis=1
    )
    incoming = with_halo(outgoing.astype(jnp.bfloat16), (("seq", 1),), rows_here).astype(
        outgoing.dtype
    )
    own_grads = own_grads + incoming[:, :rows_here] + incoming[:, 3 * rows_here :]
    sink_terms = (
        near_terms[:, 3 * rows_here :].reshape(2, 2, rows_here, width).transpose(1, 0, 2, 3)
    )
    sink_total = lax.psum(sink_terms, "seq")
    sink_mine = lax.dynamic_index_in_dim(sink_total, jnp.minimum(my_index, 1), 0, keepdims=False)
    own_grads = own_grads + jnp.where(my_index < 2, sink_mine, jnp.zeros_like(sink_mine))
    far_key_term = softmax_scale * jnp.einsum(
        "htrk,thd->hrkd", far_dscore, query_heads, preferred_element_type=jnp.float32
    )
    far_value_term = jnp.einsum(
        "htrk,thd->hrkd", far_probs, grad_heads, preferred_element_type=jnp.float32
    )
    far_terms = (
        jnp.stack([far_key_term, far_value_term], axis=2)
        .astype(jnp.bfloat16)
        .reshape(item_count, 2, rows_here, HD)
    )
    outbox = (
        jnp.zeros((devices, most_slots, 2, rows_here, HD), jnp.bfloat16)
        .at[dests, slot_rank]
        .set(far_terms)
    )
    returned = lax.all_to_all(outbox, "seq", split_axis=0, concat_axis=0, tiled=True)
    head_hot = (wanted[:, :, None] == jnp.arange(H, dtype=jnp.int32)[None, None, :]).astype(
        jnp.bfloat16
    )
    gained = jnp.einsum("nmh,nmcbd->cbhd", head_hot, returned, preferred_element_type=jnp.float32)
    own_grads = own_grads + gained.reshape(2, rows_here, width)
    return (grad_queries, own_grads[0].astype(jnp.bfloat16), own_grads[1].astype(jnp.bfloat16))


def solution(mesh):
    placed = (
        P(("groups", "seq"), None),
        P(("groups", "seq"), None),
        P(("groups", "seq"), None),
        P(("groups", "seq"), None),
        P(("groups", "seq"), None, None),
    )
    return jax.shard_map(
        per_device,
        mesh=mesh,
        in_specs=placed,
        out_specs=(
            P(("groups", "seq"), None),
            P(("groups", "seq"), None),
            P(("groups", "seq"), None),
        ),
        check_vma=False,
    )
```

profile of v0, /device:TPU:0, one launch (start us, length us, event | category | flops | bytes accessed | tf_op | source)
XLA Modules:
  0.0 459.0 jit_solution(7758403241742781614)
XLA Ops:
  8.5 2.8 scatter_fusion
  12.0 7.4 %all-to-all-start = ((s32[16,1,3]{2,1,0:T(1,128)}), s32[16,1,3]{2,1,0:T(1,128)S(1)}, u32[]{:S(2)}, u32[]{:S(2)}) async-start(s32[16,1,3]{2,1,0:T(1,128)} %copy.159), calls=%async_computation | async-start | bytes 16384 | tf_op jit(solution)/shard_map/all_to_all | solution.py:53
  21.7 4.0 all-to-all-done
  26.0 2.7 gather_fusion
  28.7 3.8 broadcast_select_fusion
  32.5 4.5 all-to-all-start.1
  48.5 2.4 constant_dynamic-update-slice_fusion.2
  50.9 169.4 %all-reduce.6.cloned.1.call-done = (bf16[2,128,2048]{1,2,0:T(8,128)(2,1)}, bf16[2,128,2048]{1,2,0:T(8,128)(2,1)}) async-done(((bf16[2,128,2048]{1,2,0:T(8,128)(2,1)}, bf16[2,128,2048]{1,2,0:T(8,128)(2,1)}), (bf16[2,128,2048]{1,2,0:T(8,128)(2,1)}, bf16[2,128,2048]{1,2,0:T(8,128)(2,1)})) %all-reduce.6.cloned.1.call-update) | async-done | bytes 2097168 | tf_op jit(solution)/shard_map/psum | solution.py:26
  220.3 2.4 constant_dynamic-update-slice_fusion.1
  222.7 2.3 constant_dynamic-update-slice_fusion
  225.0 4.6 %fusion.52 = (bf16[1,640,2048]{1,2,0:T(8,128)(2,1)}, bf16[1,640,2048]{1,2,0:T(8,128)(2,1)S(1)}) fusion(bf16[2,640,2048]{1,2,0:T(8,128)(2,1)} %constant_dynamic-update-slice_fusion), kind=kLoop, calls=%fused_computation.102 | loop fusion | bytes 10485760 | tf_op jit(solution)/shard_map/slice | solution.py:45
  229.6 3.7 select_reduce_fusion
  233.3 4.7 %gather_fusion.1 = bf16[48,2,128,128]{3,2,1,0:T(8,128)(2,1)} fusion(bf16[16,3,2,128,128]{4,3,2,1,0:T(8,128)(2,1)} %all-to-all-done.1, s32[48]{0:T(128)S(1)} %bitcast.171), kind=kCustom, calls=%fused_computation.1 | custom fusion | bytes 6291840 | tf_op jit(solution)/shard_map/gather | solution.py:62
  240.7 3.0 copy-done.2
  254.3 2.5 broadcast.125
  256.9 9.6 %scatter_fusion.1 = bf16[16,3,2,128,128]{4,3,2,1,0:T(8,128)(2,1)} fusion(bf16[16,3,2,128,128]{4,3,2,1,0:T(8,128)(2,1)} %broadcast.125, s32[48]{0:T(128)S(1)} %get-tuple-element.20, bf16[48,2,128,128]{3,2,1,0:T(8,128)(2,1)} %pad_maximum_fusion.1), kind=kCustom, calls=%fused_computation.3 | custom fusion | bytes 9437568 | tf_op jit(solution)/shard_map/scatter | solution.py:152
  266.4 4.5 all-to-all-start.2
  271.0 5.7 %fusion.1 = bf16[16,128,640]{1,2,0:T(8,128)(2,1)S(1)} fusion(f32[16,128]{1,0:T(8,128)S(1)} %fusion.29, bf16[640,16,128]{0,2,1:T(8,128)(2,1)} %bitcast.167, bf16[128,16,128]{0,2,1:T(8,128)(2,1)} %bitcast.173, f32[16,128]{1,0:T(8,128)S(1)} %add.70, f32[16,128]{1,0:T(8,128)S(1)} %max.27, f32[16,640,128]{2,1,0:T(8,128)} %get-tuple-element.32, ...), kind=kOutput, calls=%fused_computation.11 | convolution fusion | flops 344719360 | bytes 11035264 | tf_op jit(solution)/shard_map/thd,khd->htk/dot_general | solution.py:102
  278.3 3.2 multiply_bitcast_fusion
  281.5 6.0 %copy.181 = f32[640,16,128]{0,2,1:T(8,128)} copy(f32[640,16,128]{2,0,1:T(8,128)} %multiply_bitcast_fusion) | data formatting | bytes 10485760 | tf_op jit(solution)/shard_map/mul | solution.py:115
  287.4 4.1 fusion.25
  291.6 2.3 copy-done.1
  293.9 2.3 fusion.2
  296.2 5.4 %copy.183 = f32[2,256,2048]{2,1,0:T(8,128)} copy(f32[2,256,2048]{1,2,0:T(8,128)} %fusion.2) | data formatting | bytes 8388608 | tf_op jit(solution)/shard_map/slice | solution.py:133
  301.6 5.3 %copy.184 = f32[2,2,128,2048]{2,3,0,1:T(8,128)} copy(f32[2,2,128,2048]{3,2,1,0:T(8,128)} %bitcast.151) | data formatting | bytes 8388608 | tf_op jit(solution)/shard_map/reshape | solution.py:133
  307.0 4.8 %fusion = bf16[2,640,2048]{1,2,0:T(8,128)(2,1)S(1)} fusion(f32[1,640,2048]{1,2,0:T(8,128)} %bitcast.146, f32[1,640,2048]{1,2,0:T(8,128)} %bitcast.142), kind=kLoop, calls=%fused_computation.9 | loop fusion | flops 2621440 | bytes 15728640 | tf_op jit(solution)/shard_map/convert.9
  314.7 4.0 collective-permute-start.2
  318.7 2.8 fusion.22
  323.4 14.6 %all-to-all-done.2 = bf16[16,3,2,128,128]{4,3,2,1,0:T(8,128)(2,1)} async-done(((bf16[16,3,2,128,128]{4,3,2,1,0:T(8,128)(2,1)}), bf16[16,3,2,128,128]{4,3,2,1,0:T(8,128)(2,1)}, u32[]{:S(2)}, u32[]{:S(2)}) %all-to-all-start.2) | async-done | bytes 3145760 | tf_op jit(solution)/shard_map/all_to_all | solution.py:154
  338.0 5.0 %fusion.15 = f32[2,128,16,128]{3,2,1,0:T(8,128)} fusion(bf16[16,3,2,128,128]{4,3,2,1,0:T(8,128)(2,1)} %all-to-all-done.2, s32[16,3]{0,1:T(4,128)S(1)} %bitcast.178), kind=kOutput, calls=%fused_computation.37 | convolution fusion | flops 50332416 | bytes 5243072 | tf_op jit(solution)/shard_map/nmh,nmcbd->cbhd/dot_general | solution.py:158
  345.1 101.8 %all-reduce.4.cloned.1.call-done = f32[2,2,128,2048]{2,3,1,0:T(8,128)} async-done(((f32[2,2,128,2048]{2,3,1,0:T(8,128)}), f32[2,2,128,2048]{2,3,1,0:T(8,128)}) %all-reduce.4.cloned.1.call-update) | async-done | bytes 4194320 | tf_op jit(solution)/shard_map/psum | solution.py:135
  446.9 3.2 fusion.14
  (89 shorter events, 39.9 us)
Async XLA Ops:
  7.2 13.8 %copy-start.11 = (bf16[128,2048]{1,0:T(8,128)(2,1)S(1)}, bf16[128,2048]{1,0:T(8,128)(2,1)}, u32[]{:S(2)}) copy-start(bf16[128,2048]{1,0:T(8,128)(2,1)} %param.6) | copy-start | bytes 1572868
  12.0 13.7 %all-to-all-start = ((s32[16,1,3]{2,1,0:T(1,128)}), s32[16,1,3]{2,1,0:T(1,128)S(1)}, u32[]{:S(2)}, u32[]{:S(2)}) async-start(s32[16,1,3]{2,1,0:T(1,128)} %copy.159), calls=%async_computation | async-start | bytes 16384 | tf_op jit(solution)/shard_map/all_to_all | solution.py:53
  32.5 200.8 %all-to-all-start.1 = ((bf16[16,3,2,128,128]{4,3,2,1,0:T(8,128)(2,1)}), bf16[16,3,2,128,128]{4,3,2,1,0:T(8,128)(2,1)}, u32[]{:S(2)}, u32[]{:S(2)}) async-start(bf16[16,3,2,128,128]{4,3,2,1,0:T(8,128)(2,1)} %broadcast_select_fusion), calls=%async_computation.1 | async-start | bytes 6291456 | tf_op jit(solution)/shard_map/all_to_all | solution.py:55
  37.0 183.3 %all-reduce.6.cloned.1.call-start = ((), (), s32[]{:S(2)}) async-start(), calls=%async_computation.4 | async-start | bytes 4194304 | tf_op jit(solution)/shard_map/psum | solution.py:26
  37.2 4.4 collective-permute-start
  39.4 9.1 %collective-permute-start.1 = (bf16[2,128,2048]{1,2,0:T(8,128)(2,1)S(1)}, bf16[2,128,2048]{1,2,0:T(8,128)(2,1)}, u32[]{:S(2)}, u32[]{:S(2)}) collective-permute-start(bf16[2,128,2048]{1,2,0:T(8,128)(2,1)S(1)} %pad_maximum_fusion.5), channel_id=1, source_target_pairs={{1,0},{2,1},{3,2},{4,3},{5,4},{6,5},{7,6},{8,7},{9,8},{10,9},{11,1... | collective-permute-start | bytes 3145736 | tf_op jit(solution)/shard_map/ppermute | solution.py:19
  41.8 4.3 copy-start.12
  43.8 2.3 copy-start.6
  46.1 1.0 copy-start.13
  225.0 4.6 %copy-start.8 = (bf16[128,16,128]{0,2,1:T(8,128)(2,1)S(1)}, bf16[128,16,128]{0,2,1:T(8,128)(2,1)}, u32[]{:S(2)}) copy-start(bf16[128,16,128]{0,2,1:T(8,128)(2,1)} %copy.179) | copy-start | bytes 1572868
  240.1 10.0 %copy-start.3 = (bf16[48,2,128,128]{3,2,0,1:T(8,128)(2,1)}, bf16[48,2,128,128]{3,2,0,1:T(8,128)(2,1)S(1)}, u32[]{:S(2)}) copy-start(bf16[48,2,128,128]{3,2,0,1:T(8,128)(2,1)S(1)} %copy.166) | copy-start | bytes 9437188
  240.1 3.6 copy-start.2
  245.4 1.1 copy-start.14
  246.5 1.7 copy-start.10
  251.0 1.1 copy-start.7
  266.4 71.6 %all-to-all-start.2 = ((bf16[16,3,2,128,128]{4,3,2,1,0:T(8,128)(2,1)}), bf16[16,3,2,128,128]{4,3,2,1,0:T(8,128)(2,1)}, u32[]{:S(2)}, u32[]{:S(2)}) async-start(bf16[16,3,2,128,128]{4,3,2,1,0:T(8,128)(2,1)} %scatter_fusion.1), calls=%async_computation.2 | async-start | bytes 6291456 | tf_op jit(solution)/shard_map/all_to_all | solution.py:154
  270.9 7.4 %copy-start.9 = (bf16[128,16,128]{0,2,1:T(8,128)(2,1)S(1)}, bf16[128,16,128]{0,2,1:T(8,128)(2,1)}, u32[]{:S(2)}) copy-start(bf16[128,16,128]{0,2,1:T(8,128)(2,1)} %copy.179) | copy-start | bytes 1572868
  270.9 175.9 %all-reduce.4.cloned.1.call-start = ((), (), s32[]{:S(2)}) async-start(), calls=%async_computation.3 | async-start | bytes 8388608 | tf_op jit(solution)/shard_map/psum | solution.py:135
  276.7 1.6 copy-start.4
  281.5 6.0 %copy-start.15 = (bf16[128,2048]{0,1:T(8,128)(2,1)S(1)}, bf16[128,2048]{0,1:T(8,128)(2,1)}, u32[]{:S(2)}) copy-start(bf16[128,2048]{0,1:T(8,128)(2,1)} %copy.168) | copy-start | bytes 1572868
  287.4 6.5 %copy-start = (f32[640,16,128]{0,2,1:T(8,128)S(1)}, f32[640,16,128]{0,2,1:T(8,128)}, u32[]{:S(2)}) copy-start(f32[640,16,128]{0,2,1:T(8,128)} %copy.181) | copy-start | bytes 15728644
  291.6 2.3 copy-start.1
  313.4 31.7 %collective-permute-start.3 = (bf16[2,128,2048]{1,2,0:T(8,128)(2,1)}, bf16[2,128,2048]{1,2,0:T(8,128)(2,1)}, u32[]{:S(2)}, u32[]{:S(2)}) collective-permute-start(bf16[2,128,2048]{1,2,0:T(8,128)(2,1)} %get-tuple-element.23), channel_id=1, source_target_pairs={{1,0},{2,1},{3,2},{4,3},{5,4},{6,5},{7,6},{8,7},{9,8},{10,9},{11,1... | collective-permute-start | bytes 3145736 | tf_op jit(solution)/shard_map/ppermute | solution.py:19
  314.7 30.4 %collective-permute-start.2 = (bf16[2,128,2048]{1,2,0:T(8,128)(2,1)}, bf16[2,128,2048]{1,2,0:T(8,128)(2,1)}, u32[]{:S(2)}, u32[]{:S(2)}) collective-permute-start(bf16[2,128,2048]{1,2,0:T(8,128)(2,1)} %get-tuple-element.22), channel_id=1, source_target_pairs={{0,1},{1,2},{2,3},{3,4},{4,5},{5,6},{6,7},{7,8},{8,9},{9,10},{10,1... | collective-permute-start | bytes 3145736 | tf_op jit(solution)/shard_map/ppermute | solution.py:18
  318.7 2.8 copy-start.5
Sparse Core Ops, SparseCore 0:
  46.2 173.9 all-reduce.5
  307.1 139.7 all-reduce.3
where the time goes:
time: 460 us; the launch traced here: 459 us
  waiting for transfers between devices  291 us (63%)
  local copies, waits for them, and re-layouts  76.9 us (17%)
  matrix products  31.2 us (7%)
  starting transfers between devices  25.4 us (6%)
  other arithmetic  20.4 us (4%)
  between operations  14.5 us (3%)
    psum x1, waiting for transfers between devices, broadcast(): return lax.psum(block, axis)  169 us
    psum x1, waiting for transfers between devices, per_device(): sink_total = lax.psum(sink_terms, 'seq')  102 us
    unnamed x43, local copies, waits for them, and re-layouts  22.3 us
    all_to_all x1, waiting for transfers between devices, per_device(): lax.all_to_all(outbox, 'seq', split_axis=0, concat_axis=0, tiled=True)  14.6 us
    scatter x1, local copies, waits for them, and re-layouts, per_device(): outbox = jnp.zeros((devices, most_slots, 2, rows_here, HD), jnp.bfloat16)...  9.56 us
  transfers between devices with their start and end apart: 9, of which 5 were waited for; matrix products, arithmetic and copies ran while one was open for 16% of the time, Pallas kernels for 0%

commit v1 on v0

--- a/solution.py
+++ b/solution.py
@@ -50,7 +50,20 @@
     slot_rank = jnp.sum((jnp.cumsum(dest_hot, axis=0) - dest_hot) * dest_hot, axis=1)
     kv_by_head = kv_local.reshape(2, rows_here, H, HD).transpose(2, 0, 1, 3)
     requests = jnp.full((devices, most_slots), -1, jnp.int32).at[dests, slot_rank].set(item_heads)
-    wanted = lax.all_to_all(requests, "seq", split_axis=0, concat_axis=0, tiled=True)
+    step_out = jax.lax.axis_size("seq")
+    part_next = jax.lax.axis_index("seq")
+    clean, upper = (step_out, part_next)
+    state_next = requests.shape[0] // clean
+    block_last = list(requests.shape)
+    block_last[0] = state_next
+    right_arr = block_last[0]
+    block_last[0] = right_arr * clean
+    wanted = jnp.zeros(block_last, requests.dtype)
+    for it in range(clean):
+        w2 = lax.dynamic_slice_in_dim(requests, (upper ^ it) * state_next, state_next, axis=0)
+        if it:
+            w2 = jax.lax.ppermute(w2, "seq", perm=[(c, c ^ it) for c in range(clean)])
+        wanted = lax.dynamic_update_slice_in_dim(wanted, w2, (upper ^ it) * right_arr, axis=0)
     picked = kv_by_head[jnp.maximum(wanted, 0)]
     fetched = lax.all_to_all(
         jnp.where((wanted >= 0)[:, :, None, None, None], picked, jnp.zeros_like(picked)),

time: 460 us -> 478 us (1.039)
  starting transfers between devices: 25.4 us -> 40.7 us
    ppermute x0 -> x15, starting transfers between devices: none -> 22.7 us  [per_device(): w2 = jax.lax.ppermute(w2, 'seq', perm=[(c, c ^ it) for c in range(clean)])]
    all_to_all x1 -> x0, starting transfers between devices: 7.39 us -> none  [per_device(): lax.all_to_all(requests, 'seq', split_axis=0, concat_axis=0, tiled=True)]
    ppermute x0 -> x15, waiting for transfers between devices: none -> 5.07 us  [per_device(): w2 = jax.lax.ppermute(w2, 'seq', perm=[(c, c ^ it) for c in range(clean)])]
  transfers between devices with their start and end apart: 9 -> 23, of which waited for: 5 -> 6; matrix products, arithmetic and copies ran while one was open for 16% -> 16% of each run, Pallas kernels for 0% -> 0%
where the time goes in v1:
time: 478 us; the launch traced here: 477 us
  waiting for transfers between devices  291 us (61%)
  local copies, waits for them, and re-layouts  78.4 us (16%)
  starting transfers between devices  40.7 us (9%)
  matrix products  31.1 us (7%)
  other arithmetic  20.4 us (4%)
  between operations  14.7 us (3%)
    psum x1, waiting for transfers between devices, broadcast(): return lax.psum(block, axis)  169 us
    psum x1, waiting for transfers between devices, per_device(): sink_total = lax.psum(sink_terms, 'seq')  102 us
    ppermute x15, starting transfers between devices, per_device(): w2 = jax.lax.ppermute(w2, 'seq', perm=[(c, c ^ it) for c in range(clean)])  22.7 us
    unnamed x43, local copies, waits for them, and re-layouts  22.4 us
    all_to_all x1, waiting for transfers between devices, per_device(): lax.all_to_all(outbox, 'seq', split_axis=0, concat_axis=0, tiled=True)  14.4 us
    scatter x1, local copies, waits for them, and re-layouts, per_device(): outbox = jnp.zeros((devices, most_slots, 2, rows_here, HD), jnp.bfloat16)...  9.68 us
  transfers between devices with their start and end apart: 23, of which 6 were waited for; matrix products, arithmetic and copies ran while one was open for 16% of the time, Pallas kernels for 0%

profile of v1, /device:TPU:0, one launch (start us, length us, event | category | flops | bytes accessed | tf_op | source)
XLA Modules:
  0.0 476.6 jit_solution(15811468159235494592)
XLA Ops:
  8.7 2.8 scatter_fusion
  12.1 2.6 collective-permute-start.3
  19.0 2.7 collective-permute-start.7
  22.1 2.7 collective-permute-start.9
  25.1 3.6 collective-permute-start.11
  29.1 3.6 collective-permute-start.13
  33.1 4.5 collective-permute-start.15
  39.5 3.9 collective-permute-done.16
  43.7 2.7 gather_fusion
  46.4 3.8 broadcast_select_fusion
  50.2 4.5 all-to-all-start
  68.6 169.4 %all-reduce.6.cloned.1.call-done = (bf16[2,128,2048]{1,2,0:T(8,128)(2,1)}, bf16[2,128,2048]{1,2,0:T(8,128)(2,1)}) async-done(((bf16[2,128,2048]{1,2,0:T(8,128)(2,1)}, bf16[2,128,2048]{1,2,0:T(8,128)(2,1)}), (bf16[2,128,2048]{1,2,0:T(8,128)(2,1)}, bf16[2,128,2048]{1,2,0:T(8,128)(2,1)})) %all-reduce.6.cloned.1.call-update) | async-done | bytes 2097168 | tf_op jit(solution)/shard_map/psum | solution.py:26
  242.7 4.6 fusion.52
  247.3 3.7 select_reduce_fusion
  251.0 4.6 gather_fusion.1
  258.4 3.0 copy-done.2
  272.0 2.5 broadcast.111
  274.4 9.7 %scatter_fusion.1 = bf16[16,3,2,128,128]{4,3,2,1,0:T(8,128)(2,1)} fusion(bf16[16,3,2,128,128]{4,3,2,1,0:T(8,128)(2,1)} %broadcast.111, s32[48]{0:T(128)S(1)} %get-tuple-element.20, bf16[48,2,128,128]{3,2,1,0:T(8,128)(2,1)} %pad_maximum_fusion.1), kind=kCustom, calls=%fused_computation.3 | custom fusion | bytes 9437568 | tf_op jit(solution)/shard_map/scatter | solution.py:165
  284.1 4.5 all-to-all-start.1
  288.7 5.7 %fusion.1 = bf16[16,128,640]{1,2,0:T(8,128)(2,1)S(1)} fusion(f32[16,128]{1,0:T(8,128)S(1)} %fusion.29, bf16[640,16,128]{0,2,1:T(8,128)(2,1)} %bitcast.163, bf16[128,16,128]{0,2,1:T(8,128)(2,1)} %bitcast.169, f32[16,128]{1,0:T(8,128)S(1)} %add.150, f32[16,128]{1,0:T(8,128)S(1)} %max.16, f32[16,640,128]{2,1,0:T(8,128)} %get-tuple-element.48, ...), kind=kOutput, calls=%fused_computation.11 | convolution fusion | flops 344719360 | bytes 11035264 | tf_op jit(solution)/shard_map/thd,khd->htk/dot_general | solution.py:115
  295.9 3.2 multiply_bitcast_fusion
  299.1 6.0 %copy.255 = f32[640,16,128]{0,2,1:T(8,128)} copy(f32[640,16,128]{2,0,1:T(8,128)} %multiply_bitcast_fusion) | data formatting | bytes 10485760 | tf_op jit(solution)/shard_map/mul | solution.py:128
  305.2 4.1 fusion.25
  313.9 5.4 %copy.257 = f32[2,256,2048]{2,1,0:T(8,128)} copy(f32[2,256,2048]{1,2,0:T(8,128)} %fusion.2) | data formatting | bytes 8388608 | tf_op jit(solution)/shard_map/slice | solution.py:146
  319.4 5.4 %copy.258 = f32[2,2,128,2048]{2,3,0,1:T(8,128)} copy(f32[2,2,128,2048]{3,2,1,0:T(8,128)} %bitcast.147) | data formatting | bytes 8388608 | tf_op jit(solution)/shard_map/reshape | solution.py:146
  324.8 4.8 %fusion = bf16[2,640,2048]{1,2,0:T(8,128)(2,1)S(1)} fusion(f32[1,640,2048]{1,2,0:T(8,128)} %bitcast.142, f32[1,640,2048]{1,2,0:T(8,128)} %bitcast.138), kind=kLoop, calls=%fused_computation.9 | loop fusion | flops 2621440 | bytes 15728640 | tf_op jit(solution)/shard_map/convert.9
  332.5 4.0 collective-permute-start.17
  336.6 2.8 fusion.22
  341.4 14.4 %all-to-all-done.1 = bf16[16,3,2,128,128]{4,3,2,1,0:T(8,128)(2,1)} async-done(((bf16[16,3,2,128,128]{4,3,2,1,0:T(8,128)(2,1)}), bf16[16,3,2,128,128]{4,3,2,1,0:T(8,128)(2,1)}, u32[]{:S(2)}, u32[]{:S(2)}) %all-to-all-start.1) | async-done | bytes 3145760 | tf_op jit(solution)/shard_map/all_to_all | solution.py:167
  355.7 5.0 %fusion.15 = f32[2,128,16,128]{3,2,1,0:T(8,128)} fusion(bf16[16,3,2,128,128]{4,3,2,1,0:T(8,128)(2,1)} %all-to-all-done.1, s32[16,3]{0,1:T(4,128)S(1)} %copy.263), kind=kOutput, calls=%fused_computation.37 | convolution fusion | flops 50332416 | bytes 5243072 | tf_op jit(solution)/shard_map/nmh,nmcbd->cbhd/dot_general | solution.py:171
  362.8 101.7 %all-reduce.4.cloned.1.call-done = f32[2,2,128,2048]{2,3,1,0:T(8,128)} async-done(((f32[2,2,128,2048]{2,3,1,0:T(8,128)}), f32[2,2,128,2048]{2,3,1,0:T(8,128)}) %all-reduce.4.cloned.1.call-update) | async-done | bytes 4194320 | tf_op jit(solution)/shard_map/psum | solution.py:148
  464.5 3.2 fusion.14
  (149 shorter events, 56.9 us)
Async XLA Ops:
  7.2 11.0 %copy-start.11 = (bf16[128,2048]{1,0:T(8,128)(2,1)S(1)}, bf16[128,2048]{1,0:T(8,128)(2,1)}, u32[]{:S(2)}) copy-start(bf16[128,2048]{1,0:T(8,128)(2,1)} %param.6) | copy-start | bytes 1572868
  11.6 7.4 %collective-permute-start.2 = (s32[1,3]{0,1:T(4,128)S(1)}, s32[1,3]{0,1:T(4,128)S(1)}, u32[]{:S(2)}, u32[]{:S(2)}) collective-permute-start(s32[1,3]{0,1:T(4,128)S(1)} %get-tuple-element.45), channel_id=1, source_target_pairs={{0,1},{1,0},{2,3},{3,2},{4,5},{5,4},{6,7},{7,6},{8,9},{9,8},{10,11... | collective-permute-start | bytes 44 | tf_op jit(solution)/shard_map/ppermute | solution.py:65
  12.1 9.7 %collective-permute-start.3 = (s32[1,3]{0,1:T(4,128)S(1)}, s32[1,3]{0,1:T(4,128)S(1)}, u32[]{:S(2)}, u32[]{:S(2)}) collective-permute-start(s32[1,3]{0,1:T(4,128)S(1)} %get-tuple-element.44), channel_id=1, source_target_pairs={{0,2},{1,3},{2,0},{3,1},{4,6},{5,7},{6,4},{7,5},{8,10},{9,11},{10,... | collective-permute-start | bytes 44 | tf_op jit(solution)/shard_map/ppermute | solution.py:65
  14.7 7.4 %collective-permute-start.4 = (s32[1,3]{0,1:T(4,128)S(1)}, s32[1,3]{0,1:T(4,128)S(1)}, u32[]{:S(2)}, u32[]{:S(2)}) collective-permute-start(s32[1,3]{0,1:T(4,128)S(1)} %get-tuple-element.43), channel_id=1, source_target_pairs={{0,3},{1,2},{2,1},{3,0},{4,7},{5,6},{6,5},{7,4},{8,11},{9,10},{10,... | collective-permute-start | bytes 44 | tf_op jit(solution)/shard_map/ppermute | solution.py:65
  14.8 10.2 %collective-permute-start.5 = (s32[1,3]{0,1:T(4,128)S(1)}, s32[1,3]{0,1:T(4,128)S(1)}, u32[]{:S(2)}, u32[]{:S(2)}) collective-permute-start(s32[1,3]{0,1:T(4,128)S(1)} %get-tuple-element.42), channel_id=1, source_target_pairs={{0,4},{1,5},{2,6},{3,7},{4,0},{5,1},{6,2},{7,3},{8,12},{9,13},{10,... | collective-permute-start | bytes 44 | tf_op jit(solution)/shard_map/ppermute | solution.py:65
  16.6 8.6 %collective-permute-start.6 = (s32[1,3]{0,1:T(4,128)S(1)}, s32[1,3]{0,1:T(4,128)S(1)}, u32[]{:S(2)}, u32[]{:S(2)}) collective-permute-start(s32[1,3]{0,1:T(4,128)S(1)} %get-tuple-element.41), channel_id=1, source_target_pairs={{0,5},{1,4},{2,7},{3,6},{4,1},{5,0},{6,3},{7,2},{8,13},{9,12},{10,... | collective-permute-start | bytes 44 | tf_op jit(solution)/shard_map/ppermute | solution.py:65
  19.0 9.9 %collective-permute-start.7 = (s32[1,3]{0,1:T(4,128)S(1)}, s32[1,3]{0,1:T(4,128)S(1)}, u32[]{:S(2)}, u32[]{:S(2)}) collective-permute-start(s32[1,3]{0,1:T(4,128)S(1)} %get-tuple-element.40), channel_id=1, source_target_pairs={{0,6},{1,7},{2,4},{3,5},{4,2},{5,3},{6,0},{7,1},{8,14},{9,15},{10,... | collective-permute-start | bytes 44 | tf_op jit(solution)/shard_map/ppermute | solution.py:65
  21.8 7.3 %collective-permute-start.8 = (s32[1,3]{0,1:T(4,128)S(1)}, s32[1,3]{0,1:T(4,128)S(1)}, u32[]{:S(2)}, u32[]{:S(2)}) collective-permute-start(s32[1,3]{0,1:T(4,128)S(1)} %get-tuple-element.39), channel_id=1, source_target_pairs={{0,7},{1,6},{2,5},{3,4},{4,3},{5,2},{6,1},{7,0},{8,15},{9,14},{10,... | collective-permute-start | bytes 44 | tf_op jit(solution)/shard_map/ppermute | solution.py:65
  22.1 10.8 %collective-permute-start.9 = (s32[1,3]{0,1:T(4,128)S(1)}, s32[1,3]{0,1:T(4,128)S(1)}, u32[]{:S(2)}, u32[]{:S(2)}) collective-permute-start(s32[1,3]{0,1:T(4,128)S(1)} %get-tuple-element.38), channel_id=1, source_target_pairs={{0,8},{1,9},{2,10},{3,11},{4,12},{5,13},{6,14},{7,15},{8,0},{9,1},... | collective-permute-start | bytes 44 | tf_op jit(solution)/shard_map/ppermute | solution.py:65
  24.9 8.1 %collective-permute-start.10 = (s32[1,3]{0,1:T(4,128)S(1)}, s32[1,3]{0,1:T(4,128)S(1)}, u32[]{:S(2)}, u32[]{:S(2)}) collective-permute-start(s32[1,3]{0,1:T(4,128)S(1)} %get-tuple-element.37), channel_id=1, source_target_pairs={{0,9},{1,8},{2,11},{3,10},{4,13},{5,12},{6,15},{7,14},{8,1},{9,0},... | collective-permute-start | bytes 44 | tf_op jit(solution)/shard_map/ppermute | solution.py:65
  25.1 12.6 %collective-permute-start.11 = (s32[1,3]{0,1:T(4,128)S(1)}, s32[1,3]{0,1:T(4,128)S(1)}, u32[]{:S(2)}, u32[]{:S(2)}) collective-permute-start(s32[1,3]{0,1:T(4,128)S(1)} %get-tuple-element.36), channel_id=1, source_target_pairs={{0,10},{1,11},{2,8},{3,9},{4,14},{5,15},{6,12},{7,13},{8,2},{9,3},... | collective-permute-start | bytes 44 | tf_op jit(solution)/shard_map/ppermute | solution.py:65
  28.9 9.1 %collective-permute-start.12 = (s32[1,3]{0,1:T(4,128)S(1)}, s32[1,3]{0,1:T(4,128)S(1)}, u32[]{:S(2)}, u32[]{:S(2)}) collective-permute-start(s32[1,3]{0,1:T(4,128)S(1)} %get-tuple-element.35), channel_id=1, source_target_pairs={{0,11},{1,10},{2,9},{3,8},{4,15},{5,14},{6,13},{7,12},{8,3},{9,2},... | collective-permute-start | bytes 44 | tf_op jit(solution)/shard_map/ppermute | solution.py:65
  29.1 9.0 %collective-permute-start.13 = (s32[1,3]{0,1:T(4,128)S(1)}, s32[1,3]{0,1:T(4,128)S(1)}, u32[]{:S(2)}, u32[]{:S(2)}) collective-permute-start(s32[1,3]{0,1:T(4,128)S(1)} %get-tuple-element.34), channel_id=1, source_target_pairs={{0,12},{1,13},{2,14},{3,15},{4,8},{5,9},{6,10},{7,11},{8,4},{9,5},... | collective-permute-start | bytes 44 | tf_op jit(solution)/shard_map/ppermute | solution.py:65
  32.9 5.3 %collective-permute-start.14 = (s32[1,3]{0,1:T(4,128)S(1)}, s32[1,3]{0,1:T(4,128)S(1)}, u32[]{:S(2)}, u32[]{:S(2)}) collective-permute-start(s32[1,3]{0,1:T(4,128)S(1)} %get-tuple-element.33), channel_id=1, source_target_pairs={{0,13},{1,12},{2,15},{3,14},{4,9},{5,8},{6,11},{7,10},{8,5},{9,4},... | collective-permute-start | bytes 44 | tf_op jit(solution)/shard_map/ppermute | solution.py:65
  33.1 6.3 %collective-permute-start.15 = (s32[1,3]{0,1:T(4,128)S(1)}, s32[1,3]{0,1:T(4,128)S(1)}, u32[]{:S(2)}, u32[]{:S(2)}) collective-permute-start(s32[1,3]{0,1:T(4,128)S(1)} %get-tuple-element.32), channel_id=1, source_target_pairs={{0,14},{1,15},{2,12},{3,13},{4,10},{5,11},{6,8},{7,9},{8,6},{9,7},... | collective-permute-start | bytes 44 | tf_op jit(solution)/shard_map/ppermute | solution.py:65
  37.7 5.8 %collective-permute-start.16 = (s32[1,3]{0,1:T(4,128)S(1)}, s32[1,3]{0,1:T(4,128)S(1)}, u32[]{:S(2)}, u32[]{:S(2)}) collective-permute-start(s32[1,3]{0,1:T(4,128)S(1)} %get-tuple-element.31), channel_id=1, source_target_pairs={{0,15},{1,14},{2,13},{3,12},{4,11},{5,10},{6,9},{7,8},{8,7},{9,6},... | collective-permute-start | bytes 44 | tf_op jit(solution)/shard_map/ppermute | solution.py:65
  50.2 200.8 %all-to-all-start = ((bf16[16,3,2,128,128]{4,3,2,1,0:T(8,128)(2,1)}), bf16[16,3,2,128,128]{4,3,2,1,0:T(8,128)(2,1)}, u32[]{:S(2)}, u32[]{:S(2)}) async-start(bf16[16,3,2,128,128]{4,3,2,1,0:T(8,128)(2,1)} %broadcast_select_fusion), calls=%async_computation | async-start | bytes 6291456 | tf_op jit(solution)/shard_map/all_to_all | solution.py:68
  54.7 183.3 %all-reduce.6.cloned.1.call-start = ((), (), s32[]{:S(2)}) async-start(), calls=%async_computation.3 | async-start | bytes 4194304 | tf_op jit(solution)/shard_map/psum | solution.py:26
  54.8 4.4 collective-permute-start
  57.0 9.2 %collective-permute-start.1 = (bf16[2,128,2048]{1,2,0:T(8,128)(2,1)S(1)}, bf16[2,128,2048]{1,2,0:T(8,128)(2,1)}, u32[]{:S(2)}, u32[]{:S(2)}) collective-permute-start(bf16[2,128,2048]{1,2,0:T(8,128)(2,1)S(1)} %pad_maximum_fusion.5), channel_id=1, source_target_pairs={{1,0},{2,1},{3,2},{4,3},{5,4},{6,5},{7,6},{8,7},{9,8},{10,9},{11,1... | collective-permute-start | bytes 3145736 | tf_op jit(solution)/shard_map/ppermute | solution.py:19
  59.4 4.4 copy-start.12
  242.7 4.6 copy-start.8
  257.7 9.9 %copy-start.3 = (bf16[48,2,128,128]{3,2,0,1:T(8,128)(2,1)}, bf16[48,2,128,128]{3,2,0,1:T(8,128)(2,1)S(1)}, u32[]{:S(2)}) copy-start(bf16[48,2,128,128]{3,2,0,1:T(8,128)(2,1)S(1)} %copy.240) | copy-start | bytes 9437188
  257.8 3.6 copy-start.2
  284.1 71.6 %all-to-all-start.1 = ((bf16[16,3,2,128,128]{4,3,2,1,0:T(8,128)(2,1)}), bf16[16,3,2,128,128]{4,3,2,1,0:T(8,128)(2,1)}, u32[]{:S(2)}, u32[]{:S(2)}) async-start(bf16[16,3,2,128,128]{4,3,2,1,0:T(8,128)(2,1)} %scatter_fusion.1), calls=%async_computation.1 | async-start | bytes 6291456 | tf_op jit(solution)/shard_map/all_to_all | solution.py:167
  288.6 7.3 %copy-start.9 = (bf16[128,16,128]{0,2,1:T(8,128)(2,1)S(1)}, bf16[128,16,128]{0,2,1:T(8,128)(2,1)}, u32[]{:S(2)}) copy-start(bf16[128,16,128]{0,2,1:T(8,128)(2,1)} %copy.253) | copy-start | bytes 1572868
  288.6 175.9 %all-reduce.4.cloned.1.call-start = ((), (), s32[]{:S(2)}) async-start(), calls=%async_computation.2 | async-start | bytes 8388608 | tf_op jit(solution)/shard_map/psum | solution.py:148
  299.1 6.0 %copy-start.15 = (bf16[128,2048]{0,1:T(8,128)(2,1)S(1)}, bf16[128,2048]{0,1:T(8,128)(2,1)}, u32[]{:S(2)}) copy-start(bf16[128,2048]{0,1:T(8,128)(2,1)} %copy.242) | copy-start | bytes 1572868
  305.2 6.5 %copy-start = (f32[640,16,128]{0,2,1:T(8,128)S(1)}, f32[640,16,128]{0,2,1:T(8,128)}, u32[]{:S(2)}) copy-start(f32[640,16,128]{0,2,1:T(8,128)} %copy.255) | copy-start | bytes 15728644
  331.2 31.5 %collective-permute-start.18 = (bf16[2,128,2048]{1,2,0:T(8,128)(2,1)}, bf16[2,128,2048]{1,2,0:T(8,128)(2,1)}, u32[]{:S(2)}, u32[]{:S(2)}) collective-permute-start(bf16[2,128,2048]{1,2,0:T(8,128)(2,1)} %get-tuple-element.23), channel_id=1, source_target_pairs={{1,0},{2,1},{3,2},{4,3},{5,4},{6,5},{7,6},{8,7},{9,8},{10,9},{11,1... | collective-permute-start | bytes 3145736 | tf_op jit(solution)/shard_map/ppermute | solution.py:19
  332.5 30.3 %collective-permute-start.17 = (bf16[2,128,2048]{1,2,0:T(8,128)(2,1)}, bf16[2,128,2048]{1,2,0:T(8,128)(2,1)}, u32[]{:S(2)}, u32[]{:S(2)}) collective-permute-start(bf16[2,128,2048]{1,2,0:T(8,128)(2,1)} %get-tuple-element.22), channel_id=1, source_target_pairs={{0,1},{1,2},{2,3},{3,4},{4,5},{5,6},{6,7},{7,8},{8,9},{9,10},{10,1... | collective-permute-start | bytes 3145736 | tf_op jit(solution)/shard_map/ppermute | solution.py:18
  336.6 2.8 copy-start.5
  (7 other events, 11.3 us)
Sparse Core Ops, SparseCore 0:
  63.9 173.9 all-reduce.5
  324.9 139.6 all-reduce.3
